TPU v7x, 32 devices: a whole 2x2x4 slice. The times are simulated.
32 devices in a mesh: ctx: 8 (over y, x, core), qry: 4 (over z).
Axes of the slice: x: 2, y: 2, z: 4, core: 2. Of those that a mesh axis runs over, the one named last changes fastest.
Arguments:
- hist_bins: int32 [512, 16], P(('ctx', 'qry')), may hold values from 0 to 63
- hist_ranks: int32 [512], P(('ctx', 'qry')), may hold values from 0 to 511, each once
- query_bins: int32 [32768, 16], P(('ctx', 'qry')), may hold values from 0 to 63
- bin_table: bfloat16 [1024, 512], replicated, may hold values from -4.5 to 4.5
- rank_vector: bfloat16 [512], replicated, may hold values from -5 to 5
- w_query: bfloat16 [512, 512], replicated, may hold values from -5.833631 to 5.833631
- w_key: bfloat16 [512, 512], replicated, may hold values from -0.176776695 to 0.176776695
- w_value: bfloat16 [512, 512], replicated, may hold values from -0.25 to 0.25
- w_out: bfloat16 [512, 512], replicated, may hold values from -0.25 to 0.25
- w_up: bfloat16 [512, 2048], replicated, may hold values from -0.25 to 0.25
- w_down: bfloat16 [2048, 512], replicated, may hold values from -0.125 to 0.125
Outputs:
- hist_out: bfloat16 [512, 512], P(('ctx', 'qry'))
- query_out: bfloat16 [32768, 512], P(('ctx', 'qry'))
All inputs are finite; a program needn't handle non-finite values.
Results may differ from a plain program's by a relative error of at most 0.008.
Values may be sent and summed in bfloat16 or wider, within the bound.
A program may use at most 64 MiB of HBM per device.

v0:
```python
import jax
import jax.numpy as jnp
from jax import lax
from jax.sharding import PartitionSpec as P

HEADS = 8
epsilon = 1e-05


def passed_along(block, axis, distance):
    devices = range(lax.axis_size(axis))
    route = [((i - distance) % len(devices), i) for i in devices]
    return lax.ppermute(block, axis, route)


def normalize(values):
    centered = values - jnp.mean(values, axis=-1, keepdims=True)
    variance = jnp.mean(centered * centered, axis=-1, keepdims=True)
    return centered * lax.rsqrt(variance + epsilon)


def embed_bins(bin_rows, bin_table):
    bin_count = bin_table.shape[0] // bin_rows.shape[1]
    columns = lax.broadcasted_iota(jnp.int32, (1, bin_count), 1)
    pieces = [
        (bin_rows[:, feature : feature + 1] == columns).astype(jnp.bfloat16)
        for feature in range(bin_rows.shape[1])
    ]
    one_hot = jnp.concatenate(pieces, axis=1)
    return jnp.dot(one_hot, bin_table, preferred_element_type=jnp.float32)


def history_rows(bin_rows, rank_ids, bin_table, rank_vector, history_total):
    level = (2.0 * rank_ids.astype(jnp.float32) + 1.0) / history_total - 1.0
    return (
        embed_bins(bin_rows, bin_table) + level[:, None] * rank_vector.astype(jnp.float32)[None, :]
    )


def pair_move(arrived, offset):
    return passed_along(arrived, "ctx", offset)


def circulate_one(first_block, carry_state, absorb, mover, group_count):

    def advance(step_index, loop_carry):
        moving, current = loop_carry
        moving = mover(moving, 1)
        return (moving, absorb(current, moving))

    return lax.fori_loop(0, group_count - 1, advance, (first_block, carry_state))[1]


def local(
    hist_bins,
    hist_ranks,
    query_bins,
    bin_table,
    rank_vector,
    w_query,
    w_key,
    w_value,
    w_out,
    w_up,
    w_down,
):
    group_count = lax.axis_size("ctx")
    own_rows = hist_bins.shape[0]
    history_total = float(own_rows * group_count * lax.axis_size("qry"))
    own_embed = history_rows(hist_bins, hist_ranks, bin_table, rank_vector, history_total)
    all_rows = jnp.concatenate([own_embed, embed_bins(query_bins, bin_table)], axis=0)
    normed = normalize(all_rows).astype(jnp.bfloat16)
    queries = jnp.dot(normed, w_query, preferred_element_type=jnp.float32).astype(jnp.bfloat16)
    row_count = all_rows.shape[0]
    head_dim = w_query.shape[1] // HEADS
    scale = head_dim ** (-0.5)
    query_heads = queries.reshape(row_count, HEADS, head_dim)
    initial = (
        jnp.full((HEADS, row_count), -1e30, jnp.float32),
        jnp.zeros((HEADS, row_count), jnp.float32),
        jnp.zeros((HEADS, row_count, head_dim), jnp.float32),
    )

    def absorb_pair(carry_state, key_rows, value_rows):
        row_peak, row_total, summed = carry_state
        key_heads = key_rows.reshape(-1, HEADS, head_dim)
        value_heads = value_rows.reshape(-1, HEADS, head_dim)
        scores = (
            jnp.einsum("nhd,khd->hnk", query_heads, key_heads, preferred_element_type=jnp.float32)
            * scale
        )
        new_peak = jnp.maximum(row_peak, jnp.max(scores, axis=-1))
        factor = jnp.exp(row_peak - new_peak)
        weights = jnp.exp(scores - new_peak[..., None])
        row_total = row_total * factor + jnp.sum(weights, axis=-1)
        summed = summed * factor[..., None] + jnp.einsum(
            "hnk,khd->hnd",
            weights.astype(jnp.bfloat16),
            value_heads,
            preferred_element_type=jnp.float32,
        )
        return (new_peak, row_total, summed)

    history_normed = normed[:own_rows]
    key_rows = jnp.dot(history_normed, w_key, preferred_element_type=jnp.float32).astype(
        jnp.bfloat16
    )
    value_rows = jnp.dot(history_normed, w_value, preferred_element_type=jnp.float32).astype(
        jnp.bfloat16
    )
    key_pairs = jnp.stack((key_rows, value_rows))
    first_block = lax.all_gather(key_pairs, "qry", axis=1, tiled=True)

    def absorb(carry_state, arrived):
        return absorb_pair(carry_state, arrived[0], arrived[1])

    carry_state = absorb(initial, first_block)
    carry_state = circulate_one(first_block, carry_state, absorb, pair_move, group_count)
    row_peak, row_total, summed = carry_state
    attended = (
        jnp.transpose(summed / row_total[..., None], (1, 0, 2))
        .reshape(row_count, -1)
        .astype(jnp.bfloat16)
    )
    after_attention = all_rows + jnp.dot(attended, w_out, preferred_element_type=jnp.float32)
    inner = jnp.dot(
        normalize(after_attention).astype(jnp.bfloat16), w_up, preferred_element_type=jnp.float32
    )
    hidden = jax.nn.gelu(inner, approximate=True).astype(jnp.bfloat16)
    result = (after_attention + jnp.dot(hidden, w_down, preferred_element_type=jnp.float32)).astype(
        jnp.bfloat16
    )
    return (result[:own_rows], result[own_rows:])


def solution(mesh):
    return jax.shard_map(
        local,
        mesh=mesh,
        in_specs=(
            P(("ctx", "qry"), None),
            P(("ctx", "qry")),
            P(("ctx", "qry"), None),
            P(),
            P(),
            P(),
            P(),
            P(),
            P(),
            P(),
            P(),
        ),
        out_specs=(P(("ctx", "qry"), None), P(("ctx", "qry"), None)),
        check_vma=False,
    )
```

profile of v0, /device:TPU:0, one launch (start us, length us, event | category | flops | bytes accessed | tf_op | source)
XLA Modules:
  0.0 152.9 jit_solution(12912885577135275044)
XLA Ops:
  0.6 0.8 multiply_add_fusion.1
  1.5 0.7 convert_element_type.31
  2.1 1.7 %slice_reduce_fusion = (s32[16]{0:T(128)S(1)}, s32[16]{0:T(128)S(1)}, s32[16]{0:T(128)S(1)}, s32[16]{0:T(128)S(1)}, s32[16]{0:T(128)S(1)}, /*index=5*/s32[16]{0:...) fusion(s32[16,16]{1,0:T(8,128)} %param.13), kind=kLoop, calls=%fused_computation.67 | loop fusion | bytes 2048 | tf_op jit(solution)/shard_map/slice | solution.py:26
  4.6 1.5 convolution_add_fusion.4
  6.1 1.3 fusion.36
  7.7 1.0 iota_compare_fusion
  8.8 1.0 iota_compare_fusion.4
  9.8 1.0 iota_compare_fusion.6
  10.9 1.0 iota_compare_fusion.8
  11.9 1.0 iota_compare_fusion.10
  12.9 1.0 iota_compare_fusion.12
  14.0 1.0 iota_compare_fusion.14
  15.0 5.7 %concatenate.17 = pred[1024,1024]{1,0:T(32,128)(4,1)S(1)} concatenate(pred[1024,64]{1,0:T(32,128)(4,1)} %get-tuple-element.116, pred[1024,64]{1,0:T(32,128)(4,1)} %get-tuple-element.115, pred[1024,64]{1,0:T(32,128)(4,1)} %get-tuple-element.114, pred[1024,64]{1,0:T(32,128)(4,1)} %get-tuple-element.113, pred[1024,64]{1,0:T(32,128)(4,1)} %get-tuple-element.112, ...), dimensions={1} | concatenate | bytes 2097152 | tf_op jit(solution)/shard_map/concatenate | solution.py:29
  20.7 2.5 %fusion.39 = f32[1024,512]{1,0:T(8,128)S(1)} fusion(pred[1024,1024]{1,0:T(32,128)(4,1)S(1)} %concatenate.17, bf16[1024,512]{1,0:T(8,128)(2,1)} %param.16), kind=kOutput, calls=%fused_computation.112 | convolution fusion | flops 1073741824 | bytes 4194304 | tf_op jit(solution)/shard_map/dot_general | solution.py:30
  25.6 1.7 %convolution_convert_fusion = bf16[1040,512]{1,0:T(8,128)(2,1)} fusion(bf16[1040,512]{1,0:T(8,128)(2,1)S(1)} %multiply_convert_fusion.1, bf16[512,512]{1,0:T(8,128)(2,1)S(1)} %copy-done.19), kind=kOutput, calls=%fused_computation.23 | convolution fusion | flops 545792000 | bytes 2654208 | tf_op jit(solution)/shard_map/dot_general | solution.py:73
  27.3 15.2 %all_gather.3 = bf16[2,64,512]{2,1,0:T(8,128)(2,1)S(1)} all-gather(bf16[2,16,512]{2,1,0:T(8,128)(2,1)S(1)} %pad_maximum_fusion.1), channel_id=1, replica_groups=mesh['ctx'=8,'qry'=4] {'qry'}, dimensions={1}, use_global_device_ids=true | all-gather | bytes 163840 | tf_op jit(solution)/shard_map/all_gather | solution.py:112
  42.5 1.7 %copy.20 = bf16[1040,512]{0,1:T(8,128)(2,1)S(1)} copy(bf16[1040,512]{1,0:T(8,128)(2,1)} %convolution_convert_fusion) | data formatting | bytes 2129920 | tf_op jit(solution)/shard_map/convert_element_type | solution.py:73
  45.0 1.0 reshape_squeeze.6
  47.5 1.9 %convolution_add_fusion.2 = f32[8,1040,64]{1,2,0:T(8,128)} fusion(bf16[64,8,64]{0,2,1:T(8,128)(2,1)S(1)} %bitcast.52, f32[8,1040,64]{1,2,0:T(8,128)S(1)} %get-tuple-element.98, f32[8,1040]{1,0:T(8,128)S(1)} %get-tuple-element.95, f32[8,1040]{1,0:T(8,128)S(1)} %broadcast_maximum_fusion), kind=kOutput, calls=%fused_computation.19 | convolution fusion | flops 69754880 | bytes 4391936 | tf_op jit(solution)/shard_map/hnk,khd->hnd/dot_general | solution.py:96
  49.4 88.3 %while.16 = (s32[]{:T(128)}, bf16[2,64,512]{2,1,0:T(8,128)(2,1)S(1)}, f32[8,1040]{1,0:T(8,128)}, f32[8,1040]{1,0:T(8,128)}, f32[8,1040,64]{1,2,0:T(8,128)}, /*index=5*/bf16[1040,8,64]{0,2,1:T(8,128)(2,1)S(1)}, s32[]{:T(128)}) while((s32[]{:T(128)}, bf16[2,64,512]{2,1,0:T(8,128)(2,1)S(1)}, f32[8,1040]{1,0:T(8,128)}, f32[8,1040]{1,0:T(8,128)}, ...), condition=%wide.region_7.0_spmd, body=%wide.region_4.0_spmd.sunk | while | flops 140591360 | bytes 32176440 | solution.py:51
  49.4 5.3 %collective-permute-done = bf16[2,64,512]{2,1,0:T(8,128)(2,1)S(1)} collective-permute-done((bf16[2,64,512]{2,1,0:T(8,128)(2,1)S(1)}, bf16[2,64,512]{2,1,0:T(8,128)(2,1)S(1)}, u32[]{:S(2)}, u32[]{:S(2)}) %collective-permute-start) | collective-permute-done | bytes 131104 | tf_op jit(solution)/shard_map/while/body/eval_jaxpr/ppermute | solution.py:13
  54.7 0.7 fusion.65
  55.4 1.0 squeeze.7
  56.4 1.0 copy.35
  59.6 1.1 convolution_add_fusion.6
  60.7 1.4 copy-done.2
  62.1 5.3 %collective-permute-done = bf16[2,64,512]{2,1,0:T(8,128)(2,1)S(1)} collective-permute-done((bf16[2,64,512]{2,1,0:T(8,128)(2,1)S(1)}, bf16[2,64,512]{2,1,0:T(8,128)(2,1)S(1)}, u32[]{:S(2)}, u32[]{:S(2)}) %collective-permute-start) | collective-permute-done | bytes 131104 | tf_op jit(solution)/shard_map/while/body/eval_jaxpr/ppermute | solution.py:13
  67.4 0.7 fusion.65
  68.0 1.0 squeeze.7
  69.0 1.0 copy.35
  72.2 1.1 convolution_add_fusion.6
  73.3 1.4 copy-done.2
  74.7 5.3 %collective-permute-done = bf16[2,64,512]{2,1,0:T(8,128)(2,1)S(1)} collective-permute-done((bf16[2,64,512]{2,1,0:T(8,128)(2,1)S(1)}, bf16[2,64,512]{2,1,0:T(8,128)(2,1)S(1)}, u32[]{:S(2)}, u32[]{:S(2)}) %collective-permute-start) | collective-permute-done | bytes 131104 | tf_op jit(solution)/shard_map/while/body/eval_jaxpr/ppermute | solution.py:13
  80.0 0.7 fusion.65
  80.6 1.0 squeeze.7
  81.6 1.0 copy.35
  84.8 1.1 convolution_add_fusion.6
  85.9 1.4 copy-done.2
  87.3 5.3 %collective-permute-done = bf16[2,64,512]{2,1,0:T(8,128)(2,1)S(1)} collective-permute-done((bf16[2,64,512]{2,1,0:T(8,128)(2,1)S(1)}, bf16[2,64,512]{2,1,0:T(8,128)(2,1)S(1)}, u32[]{:S(2)}, u32[]{:S(2)}) %collective-permute-start) | collective-permute-done | bytes 131104 | tf_op jit(solution)/shard_map/while/body/eval_jaxpr/ppermute | solution.py:13
  92.6 0.7 fusion.65
  93.2 1.0 squeeze.7
  94.2 1.0 copy.35
  97.4 1.1 convolution_add_fusion.6
  98.5 1.4 copy-done.2
  99.9 5.3 %collective-permute-done = bf16[2,64,512]{2,1,0:T(8,128)(2,1)S(1)} collective-permute-done((bf16[2,64,512]{2,1,0:T(8,128)(2,1)S(1)}, bf16[2,64,512]{2,1,0:T(8,128)(2,1)S(1)}, u32[]{:S(2)}, u32[]{:S(2)}) %collective-permute-start) | collective-permute-done | bytes 131104 | tf_op jit(solution)/shard_map/while/body/eval_jaxpr/ppermute | solution.py:13
  105.9 1.0 squeeze.7
  106.8 1.0 copy.35
  110.0 1.1 convolution_add_fusion.6
  111.1 1.4 copy-done.2
  112.5 5.3 %collective-permute-done = bf16[2,64,512]{2,1,0:T(8,128)(2,1)S(1)} collective-permute-done((bf16[2,64,512]{2,1,0:T(8,128)(2,1)S(1)}, bf16[2,64,512]{2,1,0:T(8,128)(2,1)S(1)}, u32[]{:S(2)}, u32[]{:S(2)}) %collective-permute-start) | collective-permute-done | bytes 131104 | tf_op jit(solution)/shard_map/while/body/eval_jaxpr/ppermute | solution.py:13
  118.5 1.0 squeeze.7
  119.5 1.0 copy.35
  122.6 1.1 convolution_add_fusion.6
  123.7 1.4 copy-done.2
  125.1 5.3 %collective-permute-done = bf16[2,64,512]{2,1,0:T(8,128)(2,1)S(1)} collective-permute-done((bf16[2,64,512]{2,1,0:T(8,128)(2,1)S(1)}, bf16[2,64,512]{2,1,0:T(8,128)(2,1)S(1)}, u32[]{:S(2)}, u32[]{:S(2)}) %collective-permute-start) | collective-permute-done | bytes 131104 | tf_op jit(solution)/shard_map/while/body/eval_jaxpr/ppermute | solution.py:13
  131.1 1.0 squeeze.7
  132.1 1.0 copy.35
  135.2 1.1 convolution_add_fusion.6
  136.3 1.4 copy-done.2
  137.7 2.0 %divide_convert_fusion = bf16[8,1040,64]{1,2,0:T(8,128)(2,1)S(1)} fusion(f32[8,1040,64]{1,2,0:T(8,128)} %get-tuple-element.35, f32[8,1040]{1,0:T(8,128)} %get-tuple-element.36), kind=kLoop, calls=%fused_computation.24 | loop fusion | flops 1064960 | bytes 3228160 | tf_op jit(solution)/shard_map/convert_element_type | solution.py:123
  140.1 0.9 fusion.38
  141.0 1.3 copy-done.7
  142.8 8.4 %fusion.13 = bf16[1040,512]{1,0:T(8,128)(2,1)S(1)} fusion(f32[1040,512]{1,0:T(8,128)} %copy-done.7, bf16[2048,512]{1,0:T(8,128)(2,1)S(1)} %copy-done, bf16[512,2048]{1,0:T(8,128)(2,1)} %param.22, f32[1040]{0:T(1024)S(1)} %add_rsqrt_fusion, f32[1040]{0:T(1024)S(1)} %broadcast_multiply_fusion), kind=kOutput, calls=%fused_computation.22 | convolution fusion | flops 4383907840 | bytes 7397504 | tf_op jit(solution)/shard_map/dot_general | solution.py:130
  151.8 1.0 slice.160
  (196 shorter events, 24.3 us)
Async XLA Ops:
  0.6 142.2 %copy-start = (bf16[2048,512]{1,0:T(8,128)(2,1)S(1)}, bf16[2048,512]{1,0:T(8,128)(2,1)}, u32[]{:S(2)}) copy-start(bf16[2048,512]{1,0:T(8,128)(2,1)} %param.23) | copy-start | bytes 6291460
  6.1 17.9 %copy-start.12 = (f32[16,512]{1,0:T(8,128)}, f32[16,512]{1,0:T(8,128)S(1)}, u32[]{:S(2)}) copy-start(f32[16,512]{1,0:T(8,128)S(1)} %convolution_add_fusion.4) | copy-start | bytes 98308
  23.2 1.3 copy-start.3
  23.9 1.0 copy-start.17
  23.9 1.2 copy-start.18
  24.5 1.1 copy-start.19
  42.5 2.3 %copy-start.15 = (bf16[2,64,512]{2,1,0:T(8,128)(2,1)}, bf16[2,64,512]{2,1,0:T(8,128)(2,1)S(1)}, u32[]{:S(2)}) copy-start(bf16[2,64,512]{2,1,0:T(8,128)(2,1)S(1)} %all_gather.3) | copy-start | bytes 393220
  46.5 3.0 %copy-start.8 = (f32[8,1040]{1,0:T(8,128)}, f32[8,1040]{1,0:T(8,128)S(1)}, u32[]{:S(2)}) copy-start(f32[8,1040]{1,0:T(8,128)S(1)} %broadcast_maximum_fusion) | copy-start | bytes 99844
  47.5 1.9 %copy-start.16 = (bf16[2,64,512]{2,1,0:T(8,128)(2,1)S(1)}, bf16[2,64,512]{2,1,0:T(8,128)(2,1)}, u32[]{:S(2)}) copy-start(bf16[2,64,512]{2,1,0:T(8,128)(2,1)} %copy-done.15) | copy-start | bytes 393220
  49.4 5.3 %collective-permute-start = (bf16[2,64,512]{2,1,0:T(8,128)(2,1)S(1)}, bf16[2,64,512]{2,1,0:T(8,128)(2,1)S(1)}, u32[]{:S(2)}, u32[]{:S(2)}) collective-permute-start(bf16[2,64,512]{2,1,0:T(8,128)(2,1)S(1)} %get-tuple-element.190), channel_id=1, source_target_pairs={{28,0},{0,4},{4,8},{8,12},{12,16},{16,20},{20,24},{24,28},{29,1},{... | collective-permute-start | bytes 393224 | tf_op jit(solution)/shard_map/while/body/eval_jaxpr/ppermute | solution.py:13
  54.7 1.7 %copy-start.5 = (bf16[2,64,512]{2,1,0:T(8,128)(2,1)}, bf16[2,64,512]{2,1,0:T(8,128)(2,1)S(1)}, u32[]{:S(2)}) copy-start(bf16[2,64,512]{2,1,0:T(8,128)(2,1)S(1)} %collective-permute-done) | copy-start | bytes 393220 | tf_op jit(solution)/shard_map/while
  57.9 0.8 copy-start.10
  57.9 1.7 %copy-start.1 = (f32[8,1040,64]{1,2,0:T(8,128)S(1)}, f32[8,1040,64]{1,2,0:T(8,128)}, u32[]{:S(2)}) copy-start(f32[8,1040,64]{1,2,0:T(8,128)} %get-tuple-element.193) | copy-start | bytes 6389764 | tf_op jit(solution)/shard_map/while
  58.7 2.0 %copy-start.11 = (f32[8,1040]{1,0:T(8,128)}, f32[8,1040]{1,0:T(8,128)S(1)}, u32[]{:S(2)}) copy-start(f32[8,1040]{1,0:T(8,128)S(1)} %get-tuple-element.199) | copy-start | bytes 99844 | tf_op jit(solution)/shard_map/while
  59.5 1.1 copy-start.6
  60.6 1.4 copy-start.2
  62.1 5.3 %collective-permute-start = (bf16[2,64,512]{2,1,0:T(8,128)(2,1)S(1)}, bf16[2,64,512]{2,1,0:T(8,128)(2,1)S(1)}, u32[]{:S(2)}, u32[]{:S(2)}) collective-permute-start(bf16[2,64,512]{2,1,0:T(8,128)(2,1)S(1)} %get-tuple-element.190), channel_id=1, source_target_pairs={{28,0},{0,4},{4,8},{8,12},{12,16},{16,20},{20,24},{24,28},{29,1},{... | collective-permute-start | bytes 393224 | tf_op jit(solution)/shard_map/while/body/eval_jaxpr/ppermute | solution.py:13
  67.4 1.7 %copy-start.5 = (bf16[2,64,512]{2,1,0:T(8,128)(2,1)}, bf16[2,64,512]{2,1,0:T(8,128)(2,1)S(1)}, u32[]{:S(2)}) copy-start(bf16[2,64,512]{2,1,0:T(8,128)(2,1)S(1)} %collective-permute-done) | copy-start | bytes 393220 | tf_op jit(solution)/shard_map/while
  70.5 0.8 copy-start.10
  70.5 1.7 %copy-start.1 = (f32[8,1040,64]{1,2,0:T(8,128)S(1)}, f32[8,1040,64]{1,2,0:T(8,128)}, u32[]{:S(2)}) copy-start(f32[8,1040,64]{1,2,0:T(8,128)} %get-tuple-element.193) | copy-start | bytes 6389764 | tf_op jit(solution)/shard_map/while
  71.3 2.0 %copy-start.11 = (f32[8,1040]{1,0:T(8,128)}, f32[8,1040]{1,0:T(8,128)S(1)}, u32[]{:S(2)}) copy-start(f32[8,1040]{1,0:T(8,128)S(1)} %get-tuple-element.199) | copy-start | bytes 99844 | tf_op jit(solution)/shard_map/while
  72.2 1.1 copy-start.6
  73.3 1.4 copy-start.2
  74.7 5.3 %collective-permute-start = (bf16[2,64,512]{2,1,0:T(8,128)(2,1)S(1)}, bf16[2,64,512]{2,1,0:T(8,128)(2,1)S(1)}, u32[]{:S(2)}, u32[]{:S(2)}) collective-permute-start(bf16[2,64,512]{2,1,0:T(8,128)(2,1)S(1)} %get-tuple-element.190), channel_id=1, source_target_pairs={{28,0},{0,4},{4,8},{8,12},{12,16},{16,20},{20,24},{24,28},{29,1},{... | collective-permute-start | bytes 393224 | tf_op jit(solution)/shard_map/while/body/eval_jaxpr/ppermute | solution.py:13
  80.0 1.7 %copy-start.5 = (bf16[2,64,512]{2,1,0:T(8,128)(2,1)}, bf16[2,64,512]{2,1,0:T(8,128)(2,1)S(1)}, u32[]{:S(2)}) copy-start(bf16[2,64,512]{2,1,0:T(8,128)(2,1)S(1)} %collective-permute-done) | copy-start | bytes 393220 | tf_op jit(solution)/shard_map/while
  82.6 0.8 copy-start.9
  83.1 0.8 copy-start.10
  83.1 1.7 %copy-start.1 = (f32[8,1040,64]{1,2,0:T(8,128)S(1)}, f32[8,1040,64]{1,2,0:T(8,128)}, u32[]{:S(2)}) copy-start(f32[8,1040,64]{1,2,0:T(8,128)} %get-tuple-element.193) | copy-start | bytes 6389764 | tf_op jit(solution)/shard_map/while
  83.9 2.0 %copy-start.11 = (f32[8,1040]{1,0:T(8,128)}, f32[8,1040]{1,0:T(8,128)S(1)}, u32[]{:S(2)}) copy-start(f32[8,1040]{1,0:T(8,128)S(1)} %get-tuple-element.199) | copy-start | bytes 99844 | tf_op jit(solution)/shard_map/while
  84.8 1.1 copy-start.6
  85.9 1.4 copy-start.2
  87.3 5.3 %collective-permute-start = (bf16[2,64,512]{2,1,0:T(8,128)(2,1)S(1)}, bf16[2,64,512]{2,1,0:T(8,128)(2,1)S(1)}, u32[]{:S(2)}, u32[]{:S(2)}) collective-permute-start(bf16[2,64,512]{2,1,0:T(8,128)(2,1)S(1)} %get-tuple-element.190), channel_id=1, source_target_pairs={{28,0},{0,4},{4,8},{8,12},{12,16},{16,20},{20,24},{24,28},{29,1},{... | collective-permute-start | bytes 393224 | tf_op jit(solution)/shard_map/while/body/eval_jaxpr/ppermute | solution.py:13
  92.6 1.7 %copy-start.5 = (bf16[2,64,512]{2,1,0:T(8,128)(2,1)}, bf16[2,64,512]{2,1,0:T(8,128)(2,1)S(1)}, u32[]{:S(2)}) copy-start(bf16[2,64,512]{2,1,0:T(8,128)(2,1)S(1)} %collective-permute-done) | copy-start | bytes 393220 | tf_op jit(solution)/shard_map/while
  95.7 0.8 copy-start.10
  95.7 1.7 %copy-start.1 = (f32[8,1040,64]{1,2,0:T(8,128)S(1)}, f32[8,1040,64]{1,2,0:T(8,128)}, u32[]{:S(2)}) copy-start(f32[8,1040,64]{1,2,0:T(8,128)} %get-tuple-element.193) | copy-start | bytes 6389764 | tf_op jit(solution)/shard_map/while
  96.5 2.0 %copy-start.11 = (f32[8,1040]{1,0:T(8,128)}, f32[8,1040]{1,0:T(8,128)S(1)}, u32[]{:S(2)}) copy-start(f32[8,1040]{1,0:T(8,128)S(1)} %get-tuple-element.199) | copy-start | bytes 99844 | tf_op jit(solution)/shard_map/while
  97.4 1.1 copy-start.6
  98.5 1.4 copy-start.2
  99.9 5.3 %collective-permute-start = (bf16[2,64,512]{2,1,0:T(8,128)(2,1)S(1)}, bf16[2,64,512]{2,1,0:T(8,128)(2,1)S(1)}, u32[]{:S(2)}, u32[]{:S(2)}) collective-permute-start(bf16[2,64,512]{2,1,0:T(8,128)(2,1)S(1)} %get-tuple-element.190), channel_id=1, source_target_pairs={{28,0},{0,4},{4,8},{8,12},{12,16},{16,20},{20,24},{24,28},{29,1},{... | collective-permute-start | bytes 393224 | tf_op jit(solution)/shard_map/while/body/eval_jaxpr/ppermute | solution.py:13
  105.2 1.7 %copy-start.5 = (bf16[2,64,512]{2,1,0:T(8,128)(2,1)}, bf16[2,64,512]{2,1,0:T(8,128)(2,1)S(1)}, u32[]{:S(2)}) copy-start(bf16[2,64,512]{2,1,0:T(8,128)(2,1)S(1)} %collective-permute-done) | copy-start | bytes 393220 | tf_op jit(solution)/shard_map/while
  108.3 0.8 copy-start.10
  108.3 1.7 %copy-start.1 = (f32[8,1040,64]{1,2,0:T(8,128)S(1)}, f32[8,1040,64]{1,2,0:T(8,128)}, u32[]{:S(2)}) copy-start(f32[8,1040,64]{1,2,0:T(8,128)} %get-tuple-element.193) | copy-start | bytes 6389764 | tf_op jit(solution)/shard_map/while
  109.1 2.0 %copy-start.11 = (f32[8,1040]{1,0:T(8,128)}, f32[8,1040]{1,0:T(8,128)S(1)}, u32[]{:S(2)}) copy-start(f32[8,1040]{1,0:T(8,128)S(1)} %get-tuple-element.199) | copy-start | bytes 99844 | tf_op jit(solution)/shard_map/while
  110.0 1.1 copy-start.6
  111.1 1.4 copy-start.2
  112.5 5.3 %collective-permute-start = (bf16[2,64,512]{2,1,0:T(8,128)(2,1)S(1)}, bf16[2,64,512]{2,1,0:T(8,128)(2,1)S(1)}, u32[]{:S(2)}, u32[]{:S(2)}) collective-permute-start(bf16[2,64,512]{2,1,0:T(8,128)(2,1)S(1)} %get-tuple-element.190), channel_id=1, source_target_pairs={{28,0},{0,4},{4,8},{8,12},{12,16},{16,20},{20,24},{24,28},{29,1},{... | collective-permute-start | bytes 393224 | tf_op jit(solution)/shard_map/while/body/eval_jaxpr/ppermute | solution.py:13
  117.8 1.7 %copy-start.5 = (bf16[2,64,512]{2,1,0:T(8,128)(2,1)}, bf16[2,64,512]{2,1,0:T(8,128)(2,1)S(1)}, u32[]{:S(2)}) copy-start(bf16[2,64,512]{2,1,0:T(8,128)(2,1)S(1)} %collective-permute-done) | copy-start | bytes 393220 | tf_op jit(solution)/shard_map/while
  120.4 0.8 copy-start.9
  120.9 0.8 copy-start.10
  120.9 1.7 %copy-start.1 = (f32[8,1040,64]{1,2,0:T(8,128)S(1)}, f32[8,1040,64]{1,2,0:T(8,128)}, u32[]{:S(2)}) copy-start(f32[8,1040,64]{1,2,0:T(8,128)} %get-tuple-element.193) | copy-start | bytes 6389764 | tf_op jit(solution)/shard_map/while
  121.7 2.0 %copy-start.11 = (f32[8,1040]{1,0:T(8,128)}, f32[8,1040]{1,0:T(8,128)S(1)}, u32[]{:S(2)}) copy-start(f32[8,1040]{1,0:T(8,128)S(1)} %get-tuple-element.199) | copy-start | bytes 99844 | tf_op jit(solution)/shard_map/while
  122.6 1.1 copy-start.6
  123.7 1.4 copy-start.2
  125.1 5.3 %collective-permute-start = (bf16[2,64,512]{2,1,0:T(8,128)(2,1)S(1)}, bf16[2,64,512]{2,1,0:T(8,128)(2,1)S(1)}, u32[]{:S(2)}, u32[]{:S(2)}) collective-permute-start(bf16[2,64,512]{2,1,0:T(8,128)(2,1)S(1)} %get-tuple-element.190), channel_id=1, source_target_pairs={{28,0},{0,4},{4,8},{8,12},{12,16},{16,20},{20,24},{24,28},{29,1},{... | collective-permute-start | bytes 393224 | tf_op jit(solution)/shard_map/while/body/eval_jaxpr/ppermute | solution.py:13
  130.4 1.7 %copy-start.5 = (bf16[2,64,512]{2,1,0:T(8,128)(2,1)}, bf16[2,64,512]{2,1,0:T(8,128)(2,1)S(1)}, u32[]{:S(2)}) copy-start(bf16[2,64,512]{2,1,0:T(8,128)(2,1)S(1)} %collective-permute-done) | copy-start | bytes 393220 | tf_op jit(solution)/shard_map/while
  133.5 0.8 copy-start.10
  133.5 1.7 %copy-start.1 = (f32[8,1040,64]{1,2,0:T(8,128)S(1)}, f32[8,1040,64]{1,2,0:T(8,128)}, u32[]{:S(2)}) copy-start(f32[8,1040,64]{1,2,0:T(8,128)} %get-tuple-element.193) | copy-start | bytes 6389764 | tf_op jit(solution)/shard_map/while
  134.3 2.0 %copy-start.11 = (f32[8,1040]{1,0:T(8,128)}, f32[8,1040]{1,0:T(8,128)S(1)}, u32[]{:S(2)}) copy-start(f32[8,1040]{1,0:T(8,128)S(1)} %get-tuple-element.199) | copy-start | bytes 99844 | tf_op jit(solution)/shard_map/while
  135.2 1.1 copy-start.6
  136.3 1.4 copy-start.2
  137.7 2.3 %copy-start.4 = (f32[1024,512]{1,0:T(8,128)S(1)}, f32[1024,512]{1,0:T(8,128)}, u32[]{:S(2)}) copy-start(f32[1024,512]{1,0:T(8,128)} %copy-done.3) | copy-start | bytes 6291460
  137.7 2.3 %copy-start.13 = (f32[16,512]{1,0:T(8,128)S(1)}, f32[16,512]{1,0:T(8,128)}, u32[]{:S(2)}) copy-start(f32[16,512]{1,0:T(8,128)} %copy-done.12) | copy-start | bytes 98308
  137.7 2.4 %copy-start.14 = (bf16[512,512]{1,0:T(8,128)(2,1)S(1)}, bf16[512,512]{1,0:T(8,128)(2,1)}, u32[]{:S(2)}) copy-start(bf16[512,512]{1,0:T(8,128)(2,1)} %param.21) | copy-start | bytes 1572868
  141.0 1.4 copy-start.7
  (5 other events, 3.9 us)
where the time goes:
time: 155 us; the launch traced here: 153 us
  local copies, waits for them, and re-layouts  53.6 us (35%)
  waiting for transfers between devices  37 us (24%)
  matrix products  28.3 us (18%)
  other arithmetic  17.1 us (11%)
  blocking collectives  15.2 us (10%)
    ppermute x7, waiting for transfers between devices, passed_along(): return lax.ppermute(block, axis, route)  37 us
    while x112, local copies, waits for them, and re-layouts  18.7 us
    all_gather x1, blocking collectives, local(): first_block = lax.all_gather(key_pairs, 'qry', axis=1, tiled=True)  15.2 us
    slice x15, local copies, waits for them, and re-layouts, absorb(): return absorb_pair(carry_state, arrived[0], arrived[1])  12.1 us
    dot_general x8, matrix products, absorb_pair(): jnp.einsum('hnk,khd->hnd', weights.astype(jnp.bfloat16), value_heads, pre...  9.39 us
    dot_general x1, matrix products, local(): jnp.dot(hidden, w_down, preferred_element_type=jnp.float32)  8.4 us
    eq x16, other arithmetic, embed_bins(): bin_rows[:, feature:feature + 1] == columns  8.22 us
    squeeze x7, local copies, waits for them, and re-layouts, absorb_pair(): key_heads = key_rows.reshape(-1, HEADS, head_dim)  6.83 us
  transfers between devices with their start and end apart: 7, of which 7 were waited for; matrix products, arithmetic and copies ran while one was open for 0% of the time, Pallas kernels for 0%

commit v1 on v0

--- a/solution.py
+++ b/solution.py
@@ -109,7 +109,9 @@
         jnp.bfloat16
     )
     key_pairs = jnp.stack((key_rows, value_rows))
-    first_block = lax.all_gather(key_pairs, "qry", axis=1, tiled=True)
+    first_block = jnp.concatenate(
+        lax.all_to_all(jnp.stack([key_pairs] * lax.axis_size("qry")), "qry", 0, 0), axis=1
+    )
 
     def absorb(carry_state, arrived):
         return absorb_pair(carry_state, arrived[0], arrived[1])

time: 155 us -> 157 us (1.013)
  blocking collectives: 15.2 us -> 0 us
  starting transfers between devices: 0.02 us -> 6.34 us
  other arithmetic: 17.1 us -> 23.3 us
  matrix products: 28.3 us -> 30.9 us
  waiting for transfers between devices: 37 us -> 38.7 us
    all_gather x1 -> x0, blocking collectives: 15.2 us -> none  [local(): first_block = lax.all_gather(key_pairs, 'qry', axis=1, tiled=True)]
    all_to_all x0 -> x1, starting transfers between devices: none -> 6.32 us  [local(): lax.all_to_all(jnp.stack([key_pairs] * lax.axis_size('qry')), 'qry', 0, 0)]
    eq x16, other arithmetic: 8.22 us -> 12.3 us  [embed_bins(): bin_rows[:, feature:feature + 1] == columns]
    all_to_all x0 -> x1, waiting for transfers between devices: none -> 1.66 us  [local(): lax.all_to_all(jnp.stack([key_pairs] * lax.axis_size('qry')), 'qry', 0, 0)]
    reduce_sum x1, other arithmetic: 0.25 us -> 1.86 us  [normalize(): centered = values - jnp.mean(values, axis=-1, keepdims=True)]
  transfers between devices with their start and end apart: 7 -> 8, of which waited for: 7 -> 8; matrix products, arithmetic and copies ran while one was open for 0% -> 3% of each run, Pallas kernels for 0% -> 0%
where the time goes in v1:
time: 157 us; the launch traced here: 155 us
  local copies, waits for them, and re-layouts  53.9 us (34%)
  waiting for transfers between devices  38.7 us (25%)
  matrix products  30.9 us (20%)
  other arithmetic  23.3 us (15%)
  starting transfers between devices  6.34 us (4%)
    ppermute x7, waiting for transfers between devices, passed_along(): return lax.ppermute(block, axis, route)  37 us
    while x112, local copies, waits for them, and re-layouts  18.7 us
    eq x16, other arithmetic, embed_bins(): bin_rows[:, feature:feature + 1] == columns  12.3 us
    slice x15, local copies, waits for them, and re-layouts, absorb(): return absorb_pair(carry_state, arrived[0], arrived[1])  12.1 us
    dot_general x8, matrix products, absorb_pair(): jnp.einsum('hnk,khd->hnd', weights.astype(jnp.bfloat16), value_heads, pre...  9.47 us
    dot_general x1, matrix products, local(): jnp.dot(hidden, w_down, preferred_element_type=jnp.float32)  8.39 us
    squeeze x7, local copies, waits for them, and re-layouts, absorb_pair(): key_heads = key_rows.reshape(-1, HEADS, head_dim)  6.83 us
    all_to_all x1, starting transfers between devices, local(): lax.all_to_all(jnp.stack([key_pairs] * lax.axis_size('qry')), 'qry', 0, 0)  6.32 us
  transfers between devices with their start and end apart: 8, of which 8 were waited for; matrix products, arithmetic and copies ran while one was open for 3% of the time, Pallas kernels for 0%

profile of v1, /device:TPU:0, one launch (start us, length us, event | category | flops | bytes accessed | tf_op | source)
XLA Modules:
  0.0 154.9 jit_solution(14770151080928655582)
XLA Ops:
  0.6 1.3 multiply_add_fusion.1
  2.0 0.7 convert_element_type.31
  2.7 1.7 %slice_reduce_fusion = (s32[16]{0:T(128)S(1)}, s32[16]{0:T(128)S(1)}, s32[16]{0:T(128)S(1)}, s32[16]{0:T(128)S(1)}, s32[16]{0:T(128)S(1)}, /*index=5*/s32[16]{0:...) fusion(s32[16,16]{1,0:T(8,128)} %param.13), kind=kLoop, calls=%fused_computation.68 | loop fusion | bytes 2048 | tf_op jit(solution)/shard_map/slice | solution.py:26
  4.4 1.3 fusion.37
  10.8 1.0 iota_compare_fusion
  11.7 1.0 iota_compare_fusion.4
  12.8 1.0 iota_compare_fusion.6
  13.8 1.0 iota_compare_fusion.8
  14.9 1.0 iota_compare_fusion.10
  15.9 1.0 iota_compare_fusion.12
  16.9 1.0 iota_compare_fusion.14
  18.0 5.6 %concatenate.17 = pred[1024,1024]{1,0:T(32,128)(4,1)S(1)} concatenate(pred[1024,64]{1,0:T(32,128)(4,1)} %get-tuple-element.118, pred[1024,64]{1,0:T(32,128)(4,1)} %get-tuple-element.117, pred[1024,64]{1,0:T(32,128)(4,1)} %get-tuple-element.116, pred[1024,64]{1,0:T(32,128)(4,1)} %get-tuple-element.115, pred[1024,64]{1,0:T(32,128)(4,1)} %get-tuple-element.114, ...), dimensions={1} | concatenate | bytes 2097152 | tf_op jit(solution)/shard_map/concatenate | solution.py:29
  23.7 3.8 %fusion.40 = f32[1024,512]{1,0:T(8,128)} fusion(pred[1024,1024]{1,0:T(32,128)(4,1)S(1)} %concatenate.17, bf16[1024,512]{1,0:T(8,128)(2,1)} %param.16), kind=kOutput, calls=%fused_computation.114 | convolution fusion | flops 1073741824 | bytes 4194304 | tf_op jit(solution)/shard_map/dot_general | solution.py:30
  27.8 1.6 %convolution_add_fusion.4 = f32[16,512]{1,0:T(8,128)S(1)} fusion(pred[16,1024]{1,0:T(8,128)(4,1)S(1)} %concatenate.15, bf16[1024,512]{1,0:T(8,128)(2,1)} %param.16, f32[512]{0:T(512)S(1)} %convert_element_type.31, f32[16]{0:T(128)S(1)} %copy-done.32), kind=kOutput, calls=%fused_computation.34 | convolution fusion | flops 16793600 | bytes 1099840 | tf_op jit(solution)/shard_map/dot_general | solution.py:30
  29.4 1.9 %fusion.24 = f32[1040]{0:T(1024)S(1)} fusion(f32[1024,512]{1,0:T(8,128)} %fusion.40, f32[16,512]{1,0:T(8,128)S(1)} %convolution_add_fusion.4), kind=kLoop, calls=%fused_computation.41 | loop fusion | flops 1063920 | bytes 2134080 | tf_op jit(solution)/shard_map/reduce_sum | solution.py:17
  33.1 0.7 stack.19
  33.8 6.3 %all-to-all-start = ((bf16[4,2,16,512]{3,2,1,0:T(8,128)(2,1)}), bf16[4,2,16,512]{3,2,1,0:T(8,128)(2,1)S(1)}, u32[]{:S(2)}, u32[]{:S(2)}) async-start(bf16[4,2,16,512]{3,2,1,0:T(8,128)(2,1)} %stack.19), calls=%async_computation | async-start | bytes 262144 | tf_op jit(solution)/shard_map/all_to_all | solution.py:113
  40.1 2.7 %convolution_convert_fusion = bf16[1040,512]{1,0:T(8,128)(2,1)} fusion(bf16[1040,512]{1,0:T(8,128)(2,1)S(1)} %multiply_convert_fusion.1, bf16[512,512]{1,0:T(8,128)(2,1)} %param.18), kind=kOutput, calls=%fused_computation.23 | convolution fusion | flops 545792000 | bytes 2654208 | tf_op jit(solution)/shard_map/dot_general | solution.py:73
  42.9 1.7 %copy.24 = bf16[1040,512]{0,1:T(8,128)(2,1)S(1)} copy(bf16[1040,512]{1,0:T(8,128)(2,1)} %convolution_convert_fusion) | data formatting | bytes 2129920 | tf_op jit(solution)/shard_map/convert_element_type | solution.py:73
  44.5 1.7 %all-to-all-done = bf16[4,2,16,512]{3,2,1,0:T(8,128)(2,1)S(1)} async-done(((bf16[4,2,16,512]{3,2,1,0:T(8,128)(2,1)}), bf16[4,2,16,512]{3,2,1,0:T(8,128)(2,1)S(1)}, u32[]{:S(2)}, u32[]{:S(2)}) %all-to-all-start) | async-done | bytes 131104 | tf_op jit(solution)/shard_map/all_to_all | solution.py:113
  47.0 1.0 reshape_squeeze.6
  49.5 2.0 %convolution_add_fusion.2 = f32[8,1040,64]{1,2,0:T(8,128)} fusion(f32[8,1040,64]{1,2,0:T(8,128)S(1)} %get-tuple-element.100, f32[8,1040]{1,0:T(8,128)S(1)} %get-tuple-element.97, f32[8,1040]{1,0:T(8,128)S(1)} %broadcast_maximum_fusion, bf16[64,8,64]{2,1,0:T(8,128)(2,1)S(1)} %reshape_squeeze.7), kind=kOutput, calls=%fused_computation.19 | convolution fusion | flops 69754880 | bytes 4391936 | tf_op jit(solution)/shard_map/hnk,khd->hnd/dot_general | solution.py:96
  51.5 88.3 %while.16 = (s32[]{:T(128)}, bf16[2,64,512]{2,1,0:T(8,128)(2,1)S(1)}, f32[8,1040]{1,0:T(8,128)}, f32[8,1040]{1,0:T(8,128)}, f32[8,1040,64]{1,2,0:T(8,128)}, /*index=5*/bf16[1040,8,64]{0,2,1:T(8,128)(2,1)S(1)}, s32[]{:T(128)}) while((s32[]{:T(128)}, bf16[2,64,512]{2,1,0:T(8,128)(2,1)S(1)}, f32[8,1040]{1,0:T(8,128)}, f32[8,1040]{1,0:T(8,128)}, ...), condition=%wide.region_7.0_spmd, body=%wide.region_4.0_spmd.sunk | while | flops 140591360 | bytes 32176440 | solution.py:51
  51.5 5.3 %collective-permute-done = bf16[2,64,512]{2,1,0:T(8,128)(2,1)S(1)} collective-permute-done((bf16[2,64,512]{2,1,0:T(8,128)(2,1)S(1)}, bf16[2,64,512]{2,1,0:T(8,128)(2,1)S(1)}, u32[]{:S(2)}, u32[]{:S(2)}) %collective-permute-start) | collective-permute-done | bytes 131104 | tf_op jit(solution)/shard_map/while/body/eval_jaxpr/ppermute | solution.py:13
  56.8 0.7 fusion.65
  57.5 1.0 squeeze.7
  58.5 1.0 copy.43
  61.6 1.1 convolution_add_fusion.6
  62.7 1.4 copy-done.2
  64.1 5.3 %collective-permute-done = bf16[2,64,512]{2,1,0:T(8,128)(2,1)S(1)} collective-permute-done((bf16[2,64,512]{2,1,0:T(8,128)(2,1)S(1)}, bf16[2,64,512]{2,1,0:T(8,128)(2,1)S(1)}, u32[]{:S(2)}, u32[]{:S(2)}) %collective-permute-start) | collective-permute-done | bytes 131104 | tf_op jit(solution)/shard_map/while/body/eval_jaxpr/ppermute | solution.py:13
  70.1 1.0 squeeze.7
  71.1 1.0 copy.43
  74.2 1.1 convolution_add_fusion.6
  75.4 1.4 copy-done.2
  76.7 5.3 %collective-permute-done = bf16[2,64,512]{2,1,0:T(8,128)(2,1)S(1)} collective-permute-done((bf16[2,64,512]{2,1,0:T(8,128)(2,1)S(1)}, bf16[2,64,512]{2,1,0:T(8,128)(2,1)S(1)}, u32[]{:S(2)}, u32[]{:S(2)}) %collective-permute-start) | collective-permute-done | bytes 131104 | tf_op jit(solution)/shard_map/while/body/eval_jaxpr/ppermute | solution.py:13
  82.7 1.0 squeeze.7
  83.7 1.0 copy.43
  86.8 1.1 convolution_add_fusion.6
  88.0 1.4 copy-done.2
  89.3 5.3 %collective-permute-done = bf16[2,64,512]{2,1,0:T(8,128)(2,1)S(1)} collective-permute-done((bf16[2,64,512]{2,1,0:T(8,128)(2,1)S(1)}, bf16[2,64,512]{2,1,0:T(8,128)(2,1)S(1)}, u32[]{:S(2)}, u32[]{:S(2)}) %collective-permute-start) | collective-permute-done | bytes 131104 | tf_op jit(solution)/shard_map/while/body/eval_jaxpr/ppermute | solution.py:13
  95.3 1.0 squeeze.7
  96.3 1.0 copy.43
  99.4 1.1 convolution_add_fusion.6
  100.6 1.4 copy-done.2
  102.0 5.3 %collective-permute-done = bf16[2,64,512]{2,1,0:T(8,128)(2,1)S(1)} collective-permute-done((bf16[2,64,512]{2,1,0:T(8,128)(2,1)S(1)}, bf16[2,64,512]{2,1,0:T(8,128)(2,1)S(1)}, u32[]{:S(2)}, u32[]{:S(2)}) %collective-permute-start) | collective-permute-done | bytes 131104 | tf_op jit(solution)/shard_map/while/body/eval_jaxpr/ppermute | solution.py:13
  107.9 1.0 squeeze.7
  108.9 1.0 copy.43
  112.0 1.1 convolution_add_fusion.6
  113.2 1.4 copy-done.2
  114.6 5.3 %collective-permute-done = bf16[2,64,512]{2,1,0:T(8,128)(2,1)S(1)} collective-permute-done((bf16[2,64,512]{2,1,0:T(8,128)(2,1)S(1)}, bf16[2,64,512]{2,1,0:T(8,128)(2,1)S(1)}, u32[]{:S(2)}, u32[]{:S(2)}) %collective-permute-start) | collective-permute-done | bytes 131104 | tf_op jit(solution)/shard_map/while/body/eval_jaxpr/ppermute | solution.py:13
  120.5 1.0 squeeze.7
  121.5 1.0 copy.43
  124.7 1.1 convolution_add_fusion.6
  125.8 1.4 copy-done.2
  127.2 5.3 %collective-permute-done = bf16[2,64,512]{2,1,0:T(8,128)(2,1)S(1)} collective-permute-done((bf16[2,64,512]{2,1,0:T(8,128)(2,1)S(1)}, bf16[2,64,512]{2,1,0:T(8,128)(2,1)S(1)}, u32[]{:S(2)}, u32[]{:S(2)}) %collective-permute-start) | collective-permute-done | bytes 131104 | tf_op jit(solution)/shard_map/while/body/eval_jaxpr/ppermute | solution.py:13
  133.1 1.0 squeeze.7
  134.1 1.0 copy.43
  137.3 1.1 convolution_add_fusion.6
  138.4 1.4 copy-done.2
  139.8 2.0 %divide_convert_fusion = bf16[8,1040,64]{1,2,0:T(8,128)(2,1)S(1)} fusion(f32[8,1040,64]{1,2,0:T(8,128)} %get-tuple-element.35, f32[8,1040]{1,0:T(8,128)} %get-tuple-element.36), kind=kLoop, calls=%fused_computation.24 | loop fusion | flops 1064960 | bytes 3228160 | tf_op jit(solution)/shard_map/convert_element_type | solution.py:125
  142.2 0.9 fusion.39
  143.1 1.3 copy-done.7
  144.9 8.4 %fusion.13 = bf16[1040,512]{1,0:T(8,128)(2,1)S(1)} fusion(f32[1040,512]{1,0:T(8,128)} %copy-done.7, bf16[2048,512]{1,0:T(8,128)(2,1)S(1)} %copy-done, bf16[512,2048]{1,0:T(8,128)(2,1)} %param.22, f32[1040]{0:T(1024)S(1)} %add_rsqrt_fusion, f32[1040]{0:T(1024)S(1)} %broadcast_multiply_fusion), kind=kOutput, calls=%fused_computation.22 | convolution fusion | flops 4383907840 | bytes 7397504 | tf_op jit(solution)/shard_map/dot_general | solution.py:132
  153.9 1.0 slice.162
  (225 shorter events, 30.0 us)
Async XLA Ops:
  0.6 144.2 %copy-start = (bf16[2048,512]{1,0:T(8,128)(2,1)S(1)}, bf16[2048,512]{1,0:T(8,128)(2,1)}, u32[]{:S(2)}) copy-start(bf16[2048,512]{1,0:T(8,128)(2,1)} %param.23) | copy-start | bytes 6291460
  23.6 3.9 %copy-start.19 = (pred[16,64]{1,0:T(8,128)(4,1)S(1)}, pred[16,64]{1,0:T(8,128)(4,1)}, u32[]{:S(2)}) copy-start(pred[16,64]{1,0:T(8,128)(4,1)} %get-tuple-element.122) | copy-start | bytes 3076
  23.6 3.9 %copy-start.20 = (pred[16,64]{1,0:T(8,128)(4,1)S(1)}, pred[16,64]{1,0:T(8,128)(4,1)}, u32[]{:S(2)}) copy-start(pred[16,64]{1,0:T(8,128)(4,1)} %get-tuple-element.123) | copy-start | bytes 3076
  23.6 3.9 %copy-start.21 = (pred[16,64]{1,0:T(8,128)(4,1)S(1)}, pred[16,64]{1,0:T(8,128)(4,1)}, u32[]{:S(2)}) copy-start(pred[16,64]{1,0:T(8,128)(4,1)} %get-tuple-element.124) | copy-start | bytes 3076
  23.6 3.9 %copy-start.22 = (pred[16,64]{1,0:T(8,128)(4,1)S(1)}, pred[16,64]{1,0:T(8,128)(4,1)}, u32[]{:S(2)}) copy-start(pred[16,64]{1,0:T(8,128)(4,1)} %get-tuple-element.125) | copy-start | bytes 3076
  23.6 3.9 %copy-start.23 = (pred[16,64]{1,0:T(8,128)(4,1)S(1)}, pred[16,64]{1,0:T(8,128)(4,1)}, u32[]{:S(2)}) copy-start(pred[16,64]{1,0:T(8,128)(4,1)} %get-tuple-element.126) | copy-start | bytes 3076
  23.6 3.9 %copy-start.24 = (pred[16,64]{1,0:T(8,128)(4,1)S(1)}, pred[16,64]{1,0:T(8,128)(4,1)}, u32[]{:S(2)}) copy-start(pred[16,64]{1,0:T(8,128)(4,1)} %get-tuple-element.127) | copy-start | bytes 3076
  23.6 3.9 %copy-start.25 = (pred[16,64]{1,0:T(8,128)(4,1)S(1)}, pred[16,64]{1,0:T(8,128)(4,1)}, u32[]{:S(2)}) copy-start(pred[16,64]{1,0:T(8,128)(4,1)} %get-tuple-element.128) | copy-start | bytes 3076
  23.6 3.9 %copy-start.26 = (pred[16,64]{1,0:T(8,128)(4,1)S(1)}, pred[16,64]{1,0:T(8,128)(4,1)}, u32[]{:S(2)}) copy-start(pred[16,64]{1,0:T(8,128)(4,1)} %get-tuple-element.129) | copy-start | bytes 3076
  23.6 3.9 %copy-start.27 = (pred[16,64]{1,0:T(8,128)(4,1)S(1)}, pred[16,64]{1,0:T(8,128)(4,1)}, u32[]{:S(2)}) copy-start(pred[16,64]{1,0:T(8,128)(4,1)} %get-tuple-element.130) | copy-start | bytes 3076
  23.7 3.9 %copy-start.28 = (pred[16,64]{1,0:T(8,128)(4,1)S(1)}, pred[16,64]{1,0:T(8,128)(4,1)}, u32[]{:S(2)}) copy-start(pred[16,64]{1,0:T(8,128)(4,1)} %get-tuple-element.131) | copy-start | bytes 3076
  23.7 3.9 %copy-start.29 = (pred[16,64]{1,0:T(8,128)(4,1)S(1)}, pred[16,64]{1,0:T(8,128)(4,1)}, u32[]{:S(2)}) copy-start(pred[16,64]{1,0:T(8,128)(4,1)} %get-tuple-element.132) | copy-start | bytes 3076
  23.7 3.9 %copy-start.30 = (pred[16,64]{1,0:T(8,128)(4,1)S(1)}, pred[16,64]{1,0:T(8,128)(4,1)}, u32[]{:S(2)}) copy-start(pred[16,64]{1,0:T(8,128)(4,1)} %get-tuple-element.133) | copy-start | bytes 3076
  23.7 3.9 %copy-start.31 = (pred[16,64]{1,0:T(8,128)(4,1)S(1)}, pred[16,64]{1,0:T(8,128)(4,1)}, u32[]{:S(2)}) copy-start(pred[16,64]{1,0:T(8,128)(4,1)} %get-tuple-element.134) | copy-start | bytes 3076
  23.7 4.0 %copy-start.32 = (f32[16]{0:T(128)S(1)}, f32[16]{0:T(128)}, u32[]{:S(2)}) copy-start(f32[16]{0:T(128)} %multiply_add_fusion.1) | copy-start | bytes 196
  27.7 3.5 %copy-start.3 = (f32[1024,512]{1,0:T(8,128)S(1)}, f32[1024,512]{1,0:T(8,128)}, u32[]{:S(2)}) copy-start(f32[1024,512]{1,0:T(8,128)} %fusion.40) | copy-start | bytes 6291460
  29.4 2.4 %copy-start.12 = (f32[16,512]{1,0:T(8,128)}, f32[16,512]{1,0:T(8,128)S(1)}, u32[]{:S(2)}) copy-start(f32[16,512]{1,0:T(8,128)S(1)} %convolution_add_fusion.4) | copy-start | bytes 98308
  31.7 1.2 copy-start.16
  33.8 12.4 %all-to-all-start = ((bf16[4,2,16,512]{3,2,1,0:T(8,128)(2,1)}), bf16[4,2,16,512]{3,2,1,0:T(8,128)(2,1)S(1)}, u32[]{:S(2)}, u32[]{:S(2)}) async-start(bf16[4,2,16,512]{3,2,1,0:T(8,128)(2,1)} %stack.19), calls=%async_computation | async-start | bytes 262144 | tf_op jit(solution)/shard_map/all_to_all | solution.py:113
  48.5 3.0 %copy-start.8 = (f32[8,1040]{1,0:T(8,128)}, f32[8,1040]{1,0:T(8,128)S(1)}, u32[]{:S(2)}) copy-start(f32[8,1040]{1,0:T(8,128)S(1)} %broadcast_maximum_fusion) | copy-start | bytes 99844
  49.5 2.0 %copy-start.18 = (bf16[4,2,16,512]{3,2,0,1:T(8,128)(2,1)S(1)}, bf16[4,2,16,512]{3,2,0,1:T(8,128)(2,1)}, u32[]{:S(2)}) copy-start(bf16[4,2,16,512]{3,2,0,1:T(8,128)(2,1)} %copy-done.17) | copy-start | bytes 393220
  51.5 5.3 %collective-permute-start = (bf16[2,64,512]{2,1,0:T(8,128)(2,1)S(1)}, bf16[2,64,512]{2,1,0:T(8,128)(2,1)S(1)}, u32[]{:S(2)}, u32[]{:S(2)}) collective-permute-start(bf16[2,64,512]{2,1,0:T(8,128)(2,1)S(1)} %get-tuple-element.192), channel_id=1, source_target_pairs={{28,0},{0,4},{4,8},{8,12},{12,16},{16,20},{20,24},{24,28},{29,1},{... | collective-permute-start | bytes 393224 | tf_op jit(solution)/shard_map/while/body/eval_jaxpr/ppermute | solution.py:13
  56.8 1.7 %copy-start.5 = (bf16[2,64,512]{2,1,0:T(8,128)(2,1)}, bf16[2,64,512]{2,1,0:T(8,128)(2,1)S(1)}, u32[]{:S(2)}) copy-start(bf16[2,64,512]{2,1,0:T(8,128)(2,1)S(1)} %collective-permute-done) | copy-start | bytes 393220 | tf_op jit(solution)/shard_map/while
  59.9 1.7 %copy-start.1 = (f32[8,1040,64]{1,2,0:T(8,128)S(1)}, f32[8,1040,64]{1,2,0:T(8,128)}, u32[]{:S(2)}) copy-start(f32[8,1040,64]{1,2,0:T(8,128)} %get-tuple-element.195) | copy-start | bytes 6389764 | tf_op jit(solution)/shard_map/while
  60.7 2.0 %copy-start.11 = (f32[8,1040]{1,0:T(8,128)}, f32[8,1040]{1,0:T(8,128)S(1)}, u32[]{:S(2)}) copy-start(f32[8,1040]{1,0:T(8,128)S(1)} %get-tuple-element.201) | copy-start | bytes 99844 | tf_op jit(solution)/shard_map/while
  61.6 1.1 copy-start.6
  62.7 1.4 copy-start.2
  64.1 5.3 %collective-permute-start = (bf16[2,64,512]{2,1,0:T(8,128)(2,1)S(1)}, bf16[2,64,512]{2,1,0:T(8,128)(2,1)S(1)}, u32[]{:S(2)}, u32[]{:S(2)}) collective-permute-start(bf16[2,64,512]{2,1,0:T(8,128)(2,1)S(1)} %get-tuple-element.192), channel_id=1, source_target_pairs={{28,0},{0,4},{4,8},{8,12},{12,16},{16,20},{20,24},{24,28},{29,1},{... | collective-permute-start | bytes 393224 | tf_op jit(solution)/shard_map/while/body/eval_jaxpr/ppermute | solution.py:13
  69.4 1.7 %copy-start.5 = (bf16[2,64,512]{2,1,0:T(8,128)(2,1)}, bf16[2,64,512]{2,1,0:T(8,128)(2,1)S(1)}, u32[]{:S(2)}) copy-start(bf16[2,64,512]{2,1,0:T(8,128)(2,1)S(1)} %collective-permute-done) | copy-start | bytes 393220 | tf_op jit(solution)/shard_map/while
  72.5 1.7 %copy-start.1 = (f32[8,1040,64]{1,2,0:T(8,128)S(1)}, f32[8,1040,64]{1,2,0:T(8,128)}, u32[]{:S(2)}) copy-start(f32[8,1040,64]{1,2,0:T(8,128)} %get-tuple-element.195) | copy-start | bytes 6389764 | tf_op jit(solution)/shard_map/while
  73.3 2.0 %copy-start.11 = (f32[8,1040]{1,0:T(8,128)}, f32[8,1040]{1,0:T(8,128)S(1)}, u32[]{:S(2)}) copy-start(f32[8,1040]{1,0:T(8,128)S(1)} %get-tuple-element.201) | copy-start | bytes 99844 | tf_op jit(solution)/shard_map/while
  74.2 1.1 copy-start.6
  75.3 1.4 copy-start.2
  76.7 5.3 %collective-permute-start = (bf16[2,64,512]{2,1,0:T(8,128)(2,1)S(1)}, bf16[2,64,512]{2,1,0:T(8,128)(2,1)S(1)}, u32[]{:S(2)}, u32[]{:S(2)}) collective-permute-start(bf16[2,64,512]{2,1,0:T(8,128)(2,1)S(1)} %get-tuple-element.192), channel_id=1, source_target_pairs={{28,0},{0,4},{4,8},{8,12},{12,16},{16,20},{20,24},{24,28},{29,1},{... | collective-permute-start | bytes 393224 | tf_op jit(solution)/shard_map/while/body/eval_jaxpr/ppermute | solution.py:13
  82.0 1.7 %copy-start.5 = (bf16[2,64,512]{2,1,0:T(8,128)(2,1)}, bf16[2,64,512]{2,1,0:T(8,128)(2,1)S(1)}, u32[]{:S(2)}) copy-start(bf16[2,64,512]{2,1,0:T(8,128)(2,1)S(1)} %collective-permute-done) | copy-start | bytes 393220 | tf_op jit(solution)/shard_map/while
  85.2 1.7 %copy-start.1 = (f32[8,1040,64]{1,2,0:T(8,128)S(1)}, f32[8,1040,64]{1,2,0:T(8,128)}, u32[]{:S(2)}) copy-start(f32[8,1040,64]{1,2,0:T(8,128)} %get-tuple-element.195) | copy-start | bytes 6389764 | tf_op jit(solution)/shard_map/while
  85.9 2.0 %copy-start.11 = (f32[8,1040]{1,0:T(8,128)}, f32[8,1040]{1,0:T(8,128)S(1)}, u32[]{:S(2)}) copy-start(f32[8,1040]{1,0:T(8,128)S(1)} %get-tuple-element.201) | copy-start | bytes 99844 | tf_op jit(solution)/shard_map/while
  87.9 1.4 copy-start.2
  89.3 5.3 %collective-permute-start = (bf16[2,64,512]{2,1,0:T(8,128)(2,1)S(1)}, bf16[2,64,512]{2,1,0:T(8,128)(2,1)S(1)}, u32[]{:S(2)}, u32[]{:S(2)}) collective-permute-start(bf16[2,64,512]{2,1,0:T(8,128)(2,1)S(1)} %get-tuple-element.192), channel_id=1, source_target_pairs={{28,0},{0,4},{4,8},{8,12},{12,16},{16,20},{20,24},{24,28},{29,1},{... | collective-permute-start | bytes 393224 | tf_op jit(solution)/shard_map/while/body/eval_jaxpr/ppermute | solution.py:13
  94.6 1.7 %copy-start.5 = (bf16[2,64,512]{2,1,0:T(8,128)(2,1)}, bf16[2,64,512]{2,1,0:T(8,128)(2,1)S(1)}, u32[]{:S(2)}) copy-start(bf16[2,64,512]{2,1,0:T(8,128)(2,1)S(1)} %collective-permute-done) | copy-start | bytes 393220 | tf_op jit(solution)/shard_map/while
  97.8 1.7 %copy-start.1 = (f32[8,1040,64]{1,2,0:T(8,128)S(1)}, f32[8,1040,64]{1,2,0:T(8,128)}, u32[]{:S(2)}) copy-start(f32[8,1040,64]{1,2,0:T(8,128)} %get-tuple-element.195) | copy-start | bytes 6389764 | tf_op jit(solution)/shard_map/while
  98.5 2.0 %copy-start.11 = (f32[8,1040]{1,0:T(8,128)}, f32[8,1040]{1,0:T(8,128)S(1)}, u32[]{:S(2)}) copy-start(f32[8,1040]{1,0:T(8,128)S(1)} %get-tuple-element.201) | copy-start | bytes 99844 | tf_op jit(solution)/shard_map/while
  100.5 1.4 copy-start.2
  102.0 5.3 %collective-permute-start = (bf16[2,64,512]{2,1,0:T(8,128)(2,1)S(1)}, bf16[2,64,512]{2,1,0:T(8,128)(2,1)S(1)}, u32[]{:S(2)}, u32[]{:S(2)}) collective-permute-start(bf16[2,64,512]{2,1,0:T(8,128)(2,1)S(1)} %get-tuple-element.192), channel_id=1, source_target_pairs={{28,0},{0,4},{4,8},{8,12},{12,16},{16,20},{20,24},{24,28},{29,1},{... | collective-permute-start | bytes 393224 | tf_op jit(solution)/shard_map/while/body/eval_jaxpr/ppermute | solution.py:13
  107.2 1.7 %copy-start.5 = (bf16[2,64,512]{2,1,0:T(8,128)(2,1)}, bf16[2,64,512]{2,1,0:T(8,128)(2,1)S(1)}, u32[]{:S(2)}) copy-start(bf16[2,64,512]{2,1,0:T(8,128)(2,1)S(1)} %collective-permute-done) | copy-start | bytes 393220 | tf_op jit(solution)/shard_map/while
  110.4 1.7 %copy-start.1 = (f32[8,1040,64]{1,2,0:T(8,128)S(1)}, f32[8,1040,64]{1,2,0:T(8,128)}, u32[]{:S(2)}) copy-start(f32[8,1040,64]{1,2,0:T(8,128)} %get-tuple-element.195) | copy-start | bytes 6389764 | tf_op jit(solution)/shard_map/while
  111.2 2.0 %copy-start.11 = (f32[8,1040]{1,0:T(8,128)}, f32[8,1040]{1,0:T(8,128)S(1)}, u32[]{:S(2)}) copy-start(f32[8,1040]{1,0:T(8,128)S(1)} %get-tuple-element.201) | copy-start | bytes 99844 | tf_op jit(solution)/shard_map/while
  112.0 1.1 copy-start.6
  113.1 1.4 copy-start.2
  114.6 5.3 %collective-permute-start = (bf16[2,64,512]{2,1,0:T(8,128)(2,1)S(1)}, bf16[2,64,512]{2,1,0:T(8,128)(2,1)S(1)}, u32[]{:S(2)}, u32[]{:S(2)}) collective-permute-start(bf16[2,64,512]{2,1,0:T(8,128)(2,1)S(1)} %get-tuple-element.192), channel_id=1, source_target_pairs={{28,0},{0,4},{4,8},{8,12},{12,16},{16,20},{20,24},{24,28},{29,1},{... | collective-permute-start | bytes 393224 | tf_op jit(solution)/shard_map/while/body/eval_jaxpr/ppermute | solution.py:13
  119.8 1.7 %copy-start.5 = (bf16[2,64,512]{2,1,0:T(8,128)(2,1)}, bf16[2,64,512]{2,1,0:T(8,128)(2,1)S(1)}, u32[]{:S(2)}) copy-start(bf16[2,64,512]{2,1,0:T(8,128)(2,1)S(1)} %collective-permute-done) | copy-start | bytes 393220 | tf_op jit(solution)/shard_map/while
  123.0 1.7 %copy-start.1 = (f32[8,1040,64]{1,2,0:T(8,128)S(1)}, f32[8,1040,64]{1,2,0:T(8,128)}, u32[]{:S(2)}) copy-start(f32[8,1040,64]{1,2,0:T(8,128)} %get-tuple-element.195) | copy-start | bytes 6389764 | tf_op jit(solution)/shard_map/while
  123.8 2.0 %copy-start.11 = (f32[8,1040]{1,0:T(8,128)}, f32[8,1040]{1,0:T(8,128)S(1)}, u32[]{:S(2)}) copy-start(f32[8,1040]{1,0:T(8,128)S(1)} %get-tuple-element.201) | copy-start | bytes 99844 | tf_op jit(solution)/shard_map/while
  125.7 1.4 copy-start.2
  127.2 5.3 %collective-permute-start = (bf16[2,64,512]{2,1,0:T(8,128)(2,1)S(1)}, bf16[2,64,512]{2,1,0:T(8,128)(2,1)S(1)}, u32[]{:S(2)}, u32[]{:S(2)}) collective-permute-start(bf16[2,64,512]{2,1,0:T(8,128)(2,1)S(1)} %get-tuple-element.192), channel_id=1, source_target_pairs={{28,0},{0,4},{4,8},{8,12},{12,16},{16,20},{20,24},{24,28},{29,1},{... | collective-permute-start | bytes 393224 | tf_op jit(solution)/shard_map/while/body/eval_jaxpr/ppermute | solution.py:13
  132.5 1.7 %copy-start.5 = (bf16[2,64,512]{2,1,0:T(8,128)(2,1)}, bf16[2,64,512]{2,1,0:T(8,128)(2,1)S(1)}, u32[]{:S(2)}) copy-start(bf16[2,64,512]{2,1,0:T(8,128)(2,1)S(1)} %collective-permute-done) | copy-start | bytes 393220 | tf_op jit(solution)/shard_map/while
  135.6 1.7 %copy-start.1 = (f32[8,1040,64]{1,2,0:T(8,128)S(1)}, f32[8,1040,64]{1,2,0:T(8,128)}, u32[]{:S(2)}) copy-start(f32[8,1040,64]{1,2,0:T(8,128)} %get-tuple-element.195) | copy-start | bytes 6389764 | tf_op jit(solution)/shard_map/while
  136.4 2.0 %copy-start.11 = (f32[8,1040]{1,0:T(8,128)}, f32[8,1040]{1,0:T(8,128)S(1)}, u32[]{:S(2)}) copy-start(f32[8,1040]{1,0:T(8,128)S(1)} %get-tuple-element.201) | copy-start | bytes 99844 | tf_op jit(solution)/shard_map/while
  137.3 1.1 copy-start.6
  138.4 1.4 copy-start.2
  139.8 2.3 %copy-start.4 = (f32[1024,512]{1,0:T(8,128)S(1)}, f32[1024,512]{1,0:T(8,128)}, u32[]{:S(2)}) copy-start(f32[1024,512]{1,0:T(8,128)} %fusion.40) | copy-start | bytes 6291460
  139.8 2.3 %copy-start.13 = (f32[16,512]{1,0:T(8,128)S(1)}, f32[16,512]{1,0:T(8,128)}, u32[]{:S(2)}) copy-start(f32[16,512]{1,0:T(8,128)} %copy-done.12) | copy-start | bytes 98308
  139.8 2.4 %copy-start.14 = (bf16[512,512]{1,0:T(8,128)(2,1)S(1)}, bf16[512,512]{1,0:T(8,128)(2,1)}, u32[]{:S(2)}) copy-start(bf16[512,512]{1,0:T(8,128)(2,1)} %param.21) | copy-start | bytes 1572868
  143.0 1.4 copy-start.7
  (19 other events, 15.8 us)
